TPU v7x, 32 devices: a whole 2x2x4 slice. The times are simulated.
32 devices in a mesh: dp: 8 (over z, core), mp: 4 (over y, x).
Axes of the slice: x: 2, y: 2, z: 4, core: 2. Of those that a mesh axis runs over, the one named last changes fastest.
Arguments:
- momentum: float32 [8, 256, 5120], P('dp', 'mp'), may hold values from -60 to 60
- gradient: bfloat16 [8, 256, 5120], P('dp', 'mp'), may hold values from -60 to 60
- columns: int32 [256], replicated, may hold values from 0 to 5119, as said below
Outputs:
- update: bfloat16 [256, 5120], P('mp', 'dp')
- new_momentum: float32 [8, 256, 5120], P('dp', 'mp')
Inputs may be any that keep to these rules, and one draw needn't show every extreme that they name: `columns`: 256 distinct frequencies, 0 and 5119 always among them, in no particular order.
All inputs are finite; a program needn't handle non-finite values.
Results may differ from a plain program's by a relative error of at most 0.007.
Values may be sent and summed in bfloat16 or wider, within the bound.
A program may use at most 64 MiB of HBM per device.

v0:
```python
import math
import jax
import jax.numpy as jnp
from jax import lax
from jax.sharding import PartitionSpec as P

COLS = 5120
RANK = 256
ITERS = 5
inertia = 0.9
linear_term = 3.4445
cubic_term = -4.775
quintic_term = 2.0315


def dct_table(columns):
    positions = jnp.arange(COLS, dtype=jnp.int32)
    phase_index = (2 * positions[:, None] + 1) * columns[None, :] % (4 * COLS)
    angles = phase_index.astype(jnp.float32) * (math.pi / (2 * COLS))
    column_scale = jnp.where(columns == 0, math.sqrt(1.0 / COLS), math.sqrt(2.0 / COLS))
    return (jnp.cos(angles) * column_scale[None, :]).astype(jnp.bfloat16)


def orthogonalize(gram_matrix):
    squared_norm = jnp.trace(gram_matrix) + 1e-06
    inverse_norm = 1.0 / jnp.sqrt(squared_norm)
    identity = jnp.eye(gram_matrix.shape[0], dtype=jnp.float32)
    gram_now = gram_matrix * (inverse_norm * inverse_norm)
    mixing = identity * inverse_norm
    highest = lax.Precision.HIGHEST
    for _ in range(ITERS):
        polynomial = (
            linear_term * identity
            + cubic_term * gram_now
            + quintic_term * jnp.dot(gram_now, gram_now, precision=highest)
        )
        mixing = jnp.dot(mixing, polynomial, precision=highest)
        gram_now = jnp.dot(
            jnp.dot(polynomial, gram_now, precision=highest), polynomial, precision=highest
        )
    return mixing


def body(momentum, gradient, columns):
    highest = lax.Precision.HIGHEST
    cosines = dct_table(columns)
    current = inertia * momentum[0] + gradient[0].astype(jnp.float32)
    partial_value = jnp.dot(
        current.astype(jnp.bfloat16), cosines, preferred_element_type=jnp.float32
    )
    replica_count = lax.axis_size("dp")
    summed = lax.psum(partial_value, "dp") / replica_count
    coded_rows = summed.astype(jnp.bfloat16)
    block_rows = lax.all_gather(summed, "mp", axis=0, tiled=True)
    gram_matrix = jnp.dot(block_rows.T, block_rows, precision=highest)
    mixing = orthogonalize(gram_matrix)
    orthogonal = jnp.dot(summed, mixing, precision=highest).astype(jnp.bfloat16)
    decoded = jnp.dot(coded_rows, cosines.T, preferred_element_type=jnp.float32)
    band_width = COLS // replica_count
    band_start = lax.axis_index("dp") * band_width
    band_cosines = lax.dynamic_slice_in_dim(cosines, band_start, band_width, 0)
    direction = jnp.dot(orthogonal, band_cosines.T, preferred_element_type=jnp.float32)
    row_count = momentum.shape[1] * lax.axis_size("mp")
    update = (direction * math.sqrt(row_count * COLS / RANK)).astype(jnp.bfloat16)
    new_momentum = (current - decoded)[None]
    return (update, new_momentum)


def solution(mesh):
    return jax.shard_map(
        body,
        mesh=mesh,
        in_specs=(P("dp", "mp", None), P("dp", "mp", None), P()),
        out_specs=(P("mp", "dp"), P("dp", "mp", None)),
        check_vma=False,
    )
```

profile of v0, /device:TPU:0, one launch (start us, length us, event | category | flops | bytes accessed | tf_op | source)
XLA Modules:
  0.0 141.9 jit_solution(5607261184913191640)
XLA Ops:
  7.2 0.0 all-reduce.2.cloned.1.call-start
  7.2 0.7 compare_select_fusion
  7.9 0.0 copy-start.1
  7.9 25.8 %fusion.15 = f32[64,256]{1,0:T(8,128)} fusion(bf16[1,64,5120]{2,1,0:T(8,128)(2,1)} %param.4, f32[1,64,5120]{2,1,0:T(8,128)} %param.3, f32[256]{0:T(256)S(1)} %compare_select_fusion, s32[256]{0:T(256)} %param.5, s32[5120]{0:T(1024)S(1)} %multiply_add_fusion), kind=kOutput, calls=%fused_computation.27 | convolution fusion | flops 183500800 | bytes 2054144 | tf_op jit(solution)/shard_map/dot_general | solution.py:48
  33.7 0.0 all-reduce.2.cloned.1.call-update
  33.7 0.0 copy-done.1
  33.7 22.0 %fusion.5 = bf16[5120,256]{1,0:T(8,128)(2,1)S(1)} fusion(f32[256]{0:T(256)S(1)} %compare_select_fusion, s32[256]{0:T(256)S(1)} %copy-done.1, s32[5120]{0:T(1024)S(1)} %multiply_add_fusion), kind=kLoop, calls=%fused_computation.7 | loop fusion | flops 14417920 | bytes 2643968 | tf_op jit(solution)/shard_map/convert_element_type | solution.py:21
  55.8 35.5 %all-reduce.2.cloned.1.call-done = f32[64,256]{1,0:T(8,128)} async-done(((f32[64,256]{1,0:T(8,128)}), f32[64,256]{1,0:T(8,128)}) %all-reduce.2.cloned.1.call-update) | async-done | bytes 65552 | tf_op jit(solution)/shard_map/psum | solution.py:52
  91.3 0.8 broadcast_multiply_fusion
  92.1 9.5 %all_gather.3 = f32[256,256]{1,0:T(8,128)S(1)} all-gather(f32[64,256]{1,0:T(8,128)S(1)} %broadcast_multiply_fusion), channel_id=1, replica_groups=mesh['dp'=8,'mp'=4] {'mp'}, dimensions={0}, use_global_device_ids=true | all-gather | bytes 327680 | tf_op jit(solution)/shard_map/all_gather | solution.py:54
  101.6 1.2 select_reduce_fusion
  103.5 0.4 fusion.13
  103.9 0.4 fusion.21
  104.3 0.4 fusion.18
  104.7 0.4 fusion.39
  105.1 0.4 fusion.12
  105.5 0.4 fusion.41
  105.8 0.4 fusion.42
  106.2 0.4 fusion.11
  106.6 0.4 fusion.44
  107.0 0.4 fusion.45
  107.4 0.4 fusion.10
  107.8 0.0 copy-start
  107.8 0.4 fusion.47
  108.2 0.0 copy-start.2
  108.2 0.0 copy-start.3
  108.2 0.4 fusion.48
  108.6 0.4 fusion.9
  109.0 0.4 fusion.40
  109.4 0.4 fusion.43
  109.8 0.4 fusion.46
  110.1 0.4 fusion.49
  110.5 0.0 copy-done
  110.5 0.2 convolution_convert_fusion
  110.8 0.9 fusion.14
  111.7 0.0 copy-done.2
  111.7 0.0 copy-done.3
  111.7 23.3 %fusion = f32[1,64,5120]{2,1,0:T(8,128)} fusion(bf16[1,64,5120]{2,1,0:T(8,128)(2,1)S(1)} %copy-done.3, f32[1,64,5120]{2,1,0:T(8,128)S(1)} %copy-done.2, f32[256]{0:T(256)S(1)} %compare_select_fusion, s32[256]{0:T(256)S(1)} %copy-done.1, s32[5120]{0:T(1024)S(1)} %multiply_add_fusion, f32[64,256]{1,0:T(8,128)S(1)} %copy-done), kind=kOutput, calls=%fused_computation.2 | convolution fusion | flops 183533568 | bytes 3364864 | tf_op jit(solution)/shard_map/dot_general | solution.py:58
  (1 shorter events, 0.0 us)
Async XLA Ops:
  7.2 84.1 %all-reduce.2.cloned.1.call-start = ((), (), s32[]{:S(2)}) async-start(), calls=%async_computation | async-start | bytes 131072 | tf_op jit(solution)/shard_map/psum | solution.py:52
  7.9 25.8 %copy-start.1 = (s32[256]{0:T(256)S(1)}, s32[256]{0:T(256)}, u32[]{:S(2)}) copy-start(s32[256]{0:T(256)} %param.5) | copy-start | bytes 3076
  107.8 2.7 %copy-start = (f32[64,256]{1,0:T(8,128)S(1)}, f32[64,256]{1,0:T(8,128)}, u32[]{:S(2)}) copy-start(f32[64,256]{1,0:T(8,128)} %all-reduce.2.cloned.1.call-done) | copy-start | bytes 196612
  108.2 3.5 %copy-start.2 = (f32[1,64,5120]{2,1,0:T(8,128)S(1)}, f32[1,64,5120]{2,1,0:T(8,128)}, u32[]{:S(2)}) copy-start(f32[1,64,5120]{2,1,0:T(8,128)} %param.3) | copy-start | bytes 3932164
  108.2 3.5 %copy-start.3 = (bf16[1,64,5120]{2,1,0:T(8,128)(2,1)S(1)}, bf16[1,64,5120]{2,1,0:T(8,128)(2,1)}, u32[]{:S(2)}) copy-start(bf16[1,64,5120]{2,1,0:T(8,128)(2,1)} %param.4) | copy-start | bytes 1966084
Sparse Core Ops, SparseCore 0:
  33.8 57.4 all-reduce.1
where the time goes:
time: 142 us
  matrix products  58.3 us (41%)
  waiting for transfers between devices  35.5 us (25%)
  other arithmetic  23.6 us (17%)
  between operations  14.9 us (10%)
  blocking collectives  9.46 us (7%)
    psum x1, waiting for transfers between devices, body(): summed = lax.psum(partial_value, 'dp') / replica_count  35.5 us
    dot_general x1, matrix products, body(): jnp.dot(current.astype(jnp.bfloat16), cosines, preferred_element_type=jnp...  25.8 us
    dot_general x1, matrix products, body(): decoded = jnp.dot(coded_rows, cosines.T, preferred_element_type=jnp.float32)  23.3 us
    convert_element_type x1, other arithmetic, dct_table(): return (jnp.cos(angles) * column_scale[None, :]).astype(jnp.bfloat16)  22 us
    all_gather x1, blocking collectives, body(): block_rows = lax.all_gather(summed, 'mp', axis=0, tiled=True)  9.46 us
  transfers between devices with their start and end apart: 1, of which 1 were waited for; matrix products, arithmetic and copies ran while one was open for 16% of the time, Pallas kernels for 0%

commit v1 on v0

--- a/solution.py
+++ b/solution.py
@@ -51,7 +51,14 @@
     replica_count = lax.axis_size("dp")
     summed = lax.psum(partial_value, "dp") / replica_count
     coded_rows = summed.astype(jnp.bfloat16)
-    block_rows = lax.all_gather(summed, "mp", axis=0, tiled=True)
+    ways, here, hop = (lax.axis_size("mp"), lax.axis_index("mp"), summed.shape[0])
+    line, have = (summed, 1)
+    while have < ways:
+        line = jnp.concatenate(
+            [line, lax.ppermute(line, "mp", [(d, (d - have) % ways) for d in range(ways)])], axis=0
+        )
+        have = 2 * have
+    block_rows = jnp.roll(line, here * hop, axis=0)
     gram_matrix = jnp.dot(block_rows.T, block_rows, precision=highest)
     mixing = orthogonalize(gram_matrix)
     orthogonal = jnp.dot(summed, mixing, precision=highest).astype(jnp.bfloat16)

time: 142 us -> 159 us (1.12)
  waiting for transfers between devices: 35.5 us -> 57.6 us
  blocking collectives: 9.46 us -> 0 us
  starting transfers between devices: 0.04 us -> 3.09 us
    psum x1, waiting for transfers between devices: 35.5 us -> 57.6 us  [body(): summed = lax.psum(partial_value, 'dp') / replica_count]
    all_gather x1 -> x0, blocking collectives: 9.46 us -> none  [body(): block_rows = lax.all_gather(summed, 'mp', axis=0, tiled=True)]
    ppermute x0 -> x2, starting transfers between devices: none -> 3.05 us  [body(): lax.ppermute(line, 'mp', [(d, (d - have) % ways) for d in range(ways)])]
  transfers between devices with their start and end apart: 1 -> 3, of which waited for: 1 -> 1; matrix products, arithmetic and copies ran while one was open for 16% -> 29% of each run, Pallas kernels for 0% -> 0%
where the time goes in v1:
time: 159 us
  matrix products  59.3 us (37%)
  waiting for transfers between devices  57.6 us (36%)
  other arithmetic  23.7 us (15%)
  between operations  15 us (9%)
  starting transfers between devices  3.09 us (2%)
    psum x1, waiting for transfers between devices, body(): summed = lax.psum(partial_value, 'dp') / replica_count  57.6 us
    dot_general x1, matrix products, body(): jnp.dot(current.astype(jnp.bfloat16), cosines, preferred_element_type=jnp...  25.8 us
    dot_general x1, matrix products, body(): decoded = jnp.dot(coded_rows, cosines.T, preferred_element_type=jnp.float32)  24.3 us
    convert_element_type x1, other arithmetic, dct_table(): return (jnp.cos(angles) * column_scale[None, :]).astype(jnp.bfloat16)  22 us
  transfers between devices with their start and end apart: 3, of which 1 were waited for; matrix products, arithmetic and copies ran while one was open for 29% of the time, Pallas kernels for 0%

profile of v1, /device:TPU:0, one launch (start us, length us, event | category | flops | bytes accessed | tf_op | source)
XLA Modules:
  0.0 158.7 jit_solution(7855982082719353692)
XLA Ops:
  7.2 0.0 all-reduce.2.cloned.1.call-start
  7.2 0.7 compare_select_fusion
  7.9 0.0 copy-start.1
  7.9 25.8 %fusion.15 = f32[64,256]{1,0:T(8,128)} fusion(bf16[1,64,5120]{2,1,0:T(8,128)(2,1)} %param.4, f32[1,64,5120]{2,1,0:T(8,128)} %param.3, f32[256]{0:T(256)S(1)} %compare_select_fusion, s32[256]{0:T(256)} %param.5, s32[5120]{0:T(1024)S(1)} %multiply_add_fusion), kind=kOutput, calls=%fused_computation.27 | convolution fusion | flops 183500800 | bytes 2054144 | tf_op jit(solution)/shard_map/dot_general | solution.py:48
  33.7 0.0 all-reduce.2.cloned.1.call-update
  33.7 57.6 %all-reduce.2.cloned.1.call-done = f32[64,256]{1,0:T(8,128)} async-done(((f32[64,256]{1,0:T(8,128)}), f32[64,256]{1,0:T(8,128)}) %all-reduce.2.cloned.1.call-update) | async-done | bytes 65552 | tf_op jit(solution)/shard_map/psum | solution.py:52
  91.3 0.0 copy-start
  91.3 0.9 broadcast_multiply_fusion
  92.2 2.4 %collective-permute-start = (f32[64,256]{1,0:T(8,128)S(1)}, f32[64,256]{1,0:T(8,128)S(1)}, u32[]{:S(2)}, u32[]{:S(2)}) collective-permute-start(f32[64,256]{1,0:T(8,128)S(1)} %get-tuple-element.2), channel_id=1, source_target_pairs={{0,3},{1,0},{2,1},{3,2},{4,7},{5,4},{6,5},{7,6},{8,11},{9,8},{10,9... | collective-permute-start | bytes 196616 | tf_op jit(solution)/shard_map/ppermute | solution.py:58
  94.7 0.0 copy-done.1
  94.7 22.0 %fusion.5 = bf16[5120,256]{1,0:T(8,128)(2,1)S(1)} fusion(f32[256]{0:T(256)S(1)} %compare_select_fusion, s32[256]{0:T(256)S(1)} %copy-done.1, s32[5120]{0:T(1024)S(1)} %multiply_add_fusion), kind=kLoop, calls=%fused_computation.7 | loop fusion | flops 14417920 | bytes 2643968 | tf_op jit(solution)/shard_map/convert_element_type | solution.py:21
  116.7 0.0 collective-permute-done
  116.7 0.6 collective-permute-start.1
  117.4 0.0 copy-done
  117.4 24.3 %fusion = f32[1,64,5120]{2,1,0:T(8,128)} fusion(bf16[1,64,5120]{2,1,0:T(8,128)(2,1)} %param.4, f32[1,64,5120]{2,1,0:T(8,128)} %param.3, f32[256]{0:T(256)S(1)} %compare_select_fusion, s32[256]{0:T(256)S(1)} %copy-done.1, s32[5120]{0:T(1024)S(1)} %multiply_add_fusion, f32[64,256]{1,0:T(8,128)S(1)} %copy-done), kind=kOutput, calls=%fused_computation.2 | convolution fusion | flops 183533568 | bytes 3364864 | tf_op jit(solution)/shard_map/dot_general | solution.py:65
  141.7 0.0 collective-permute-done.1
  141.8 1.2 select_reduce_fusion
  143.7 0.4 fusion.13
  144.1 0.4 fusion.23
  144.5 0.4 fusion.18
  144.9 0.4 fusion.42
  145.3 0.4 fusion.12
  145.7 0.4 fusion.44
  146.0 0.4 fusion.45
  146.4 0.4 fusion.11
  146.8 0.4 fusion.47
  147.2 0.4 fusion.48
  147.6 0.4 fusion.10
  148.0 0.4 fusion.50
  148.4 0.4 fusion.51
  148.8 0.4 fusion.9
  149.1 0.4 fusion.43
  149.5 0.4 fusion.46
  149.9 0.4 fusion.49
  150.3 0.4 fusion.52
  150.7 0.2 convolution_convert_fusion
  150.9 0.9 fusion.14
  (7 shorter events, 0.1 us)
Async XLA Ops:
  7.2 84.1 %all-reduce.2.cloned.1.call-start = ((), (), s32[]{:S(2)}) async-start(), calls=%async_computation | async-start | bytes 131072 | tf_op jit(solution)/shard_map/psum | solution.py:52
  7.9 86.8 %copy-start.1 = (s32[256]{0:T(256)S(1)}, s32[256]{0:T(256)}, u32[]{:S(2)}) copy-start(s32[256]{0:T(256)} %param.5) | copy-start | bytes 3076
  91.3 26.1 %copy-start = (f32[64,256]{1,0:T(8,128)S(1)}, f32[64,256]{1,0:T(8,128)}, u32[]{:S(2)}) copy-start(f32[64,256]{1,0:T(8,128)} %all-reduce.2.cloned.1.call-done) | copy-start | bytes 196612
  92.2 24.5 %collective-permute-start = (f32[64,256]{1,0:T(8,128)S(1)}, f32[64,256]{1,0:T(8,128)S(1)}, u32[]{:S(2)}, u32[]{:S(2)}) collective-permute-start(f32[64,256]{1,0:T(8,128)S(1)} %get-tuple-element.2), channel_id=1, source_target_pairs={{0,3},{1,0},{2,1},{3,2},{4,7},{5,4},{6,5},{7,6},{8,11},{9,8},{10,9... | collective-permute-start | bytes 196616 | tf_op jit(solution)/shard_map/ppermute | solution.py:58
  116.7 25.0 %collective-permute-start.1 = (f32[128,256]{1,0:T(8,128)S(1)}, f32[128,256]{1,0:T(8,128)S(1)}, u32[]{:S(2)}, u32[]{:S(2)}) collective-permute-start(f32[128,256]{1,0:T(8,128)S(1)} %pad_maximum_fusion), channel_id=1, source_target_pairs={{0,2},{1,3},{2,0},{3,1},{4,6},{5,7},{6,4},{7,5},{8,10},{9,11},{10,... | collective-permute-start | bytes 393224 | tf_op jit(solution)/shard_map/ppermute | solution.py:58
Sparse Core Ops, SparseCore 0:
  33.8 57.4 all-reduce.1
